TPU v7x, 32 devices: a whole 2x2x4 slice. The times are simulated.
32 devices in a mesh: dp: 4 (over x, core), sx: 2 (over y), sy: 4 (over z).
Axes of the slice: x: 2, y: 2, z: 4, core: 2. Of those that a mesh axis runs over, the one named last changes fastest.
Arguments:
- activations: bfloat16 [4, 16, 16, 2048], P('dp', 'sx', 'sy'), may hold values from -6 to 6
- preact: bfloat16 [4, 16, 16, 4096], P('dp', 'sx', 'sy'), may hold values from -6 to 6
- pooled_grad: bfloat16 [4, 8, 8, 2048], P('dp', 'sx', 'sy'), may hold values from -12 to 12
- weights: bfloat16 [27, 64, 128], replicated, may hold values from -0.109375 to 0.109375
Outputs:
- input_grad: bfloat16 [4, 16, 16, 2048], P('dp', 'sx', 'sy')
- weight_grad: float32 [27, 64, 128], replicated
- bias_grad: float32 [128], replicated
All inputs are finite; a program needn't handle non-finite values.
Results may differ from a plain program's by a relative error of at most 0.0021.
Values may be sent and summed in bfloat16 or wider, within the bound.
A program may use at most 64 MiB of HBM per device.

v0:
```python
import jax
import jax.numpy as jnp
from jax import lax
from jax.sharding import PartitionSpec as P

stencil_offsets = [(ox, oy, oz) for ox in (-1, 0, 1) for oy in (-1, 0, 1) for oz in (-1, 0, 1)]


def extended(block, sides, width):
    for axis, dim in sides:
        count = lax.axis_size(axis)
        forward = [(i, i + 1) for i in range(count - 1)]
        backward = [(target, source) for source, target in forward]
        low = lax.ppermute(
            lax.slice_in_dim(block, block.shape[dim] - width, None, axis=dim), axis, forward
        )
        high = lax.ppermute(lax.slice_in_dim(block, 0, width, axis=dim), axis, backward)
        block = jnp.concatenate([low, block, high], axis=dim)
    return block


def widen_depth(widened, cells_x, cells_y, cells_z, channels):
    count = widened.shape[0]
    shaped = widened.reshape(count, cells_x + 2, cells_y + 2, cells_z, channels)
    return jnp.pad(shaped, ((0, 0), (0, 0), (0, 0), (1, 1), (0, 0)))


def shifted(shaped, offset, sign, cells_x, cells_y, cells_z, channels):
    ox, oy, oz = offset
    piece = shaped[
        :,
        1 + sign * ox : 1 + sign * ox + cells_x,
        1 + sign * oy : 1 + sign * oy + cells_y,
        1 + sign * oz : 1 + sign * oz + cells_z,
        :,
    ]
    return piece.reshape(-1, channels)


def on_device(activations, preact, pooled_grad, weights):
    samples, cells_x, cells_y, flat_in = activations.shape
    chan_in = weights.shape[1]
    chan_out = weights.shape[2]
    cells_z = flat_in // chan_in
    upper = pooled_grad.reshape(samples, cells_x // 2, cells_y // 2, cells_z // 2, chan_out)
    grad_act = (
        jnp.repeat(jnp.repeat(jnp.repeat(upper, 2, 1), 2, 2), 2, 3).astype(jnp.float32) * 0.125
    )
    slope = jnp.where(
        preact.reshape(samples, cells_x, cells_y, cells_z, chan_out) > 0, 1.0, 0.3
    ).astype(jnp.float32)
    gate_grad = (
        (grad_act * slope)
        .astype(jnp.bfloat16)
        .reshape(samples, cells_x, cells_y, cells_z * chan_out)
    )
    grad_wide = extended(gate_grad, (("sx", 1), ("sy", 2)), 1)
    grad_shaped = widen_depth(grad_wide, cells_x, cells_y, cells_z, chan_out)
    grad_flat = gate_grad.reshape(-1, chan_out)
    act_flat = activations.reshape(-1, chan_in)
    contract = (((0,), (0,)), ((), ()))
    backward = (((1,), (1,)), ((), ()))
    act_wide = extended(activations, (("sx", 1), ("sy", 2)), 1)
    act_shaped = widen_depth(act_wide, cells_x, cells_y, cells_z, chan_in)
    input_acc = jnp.zeros((act_flat.shape[0], chan_in), jnp.float32)
    terms = []
    for index, offset in enumerate(stencil_offsets):
        moved = shifted(grad_shaped, offset, -1, cells_x, cells_y, cells_z, chan_out)
        input_acc = input_acc + lax.dot_general(
            moved, weights[index], backward, preferred_element_type=jnp.float32
        )
        act_moved = shifted(act_shaped, offset, 1, cells_x, cells_y, cells_z, chan_in)
        terms.append(
            lax.dot_general(act_moved, grad_flat, contract, preferred_element_type=jnp.float32)
        )
    input_grad = input_acc.astype(jnp.bfloat16).reshape(
        samples, cells_x, cells_y, cells_z * chan_in
    )
    weight_sum = jnp.stack(terms, axis=0).reshape(27 * chan_in, chan_out)
    bias_sum = jnp.sum(grad_flat.astype(jnp.float32), axis=0)[None, :]
    weight_total, bias_total = lax.psum((weight_sum, bias_sum), ("dp", "sx", "sy"))
    total_samples = samples * lax.axis_size("dp")
    weight_grad = (weight_total / total_samples).reshape(27, chan_in, chan_out)
    bias_grad = bias_total[0] / total_samples
    return (input_grad, weight_grad, bias_grad)


def solution(mesh):
    placed = (P("dp", "sx", "sy", None), P("dp", "sx", "sy", None), P("dp", "sx", "sy", None), P())
    return jax.shard_map(
        on_device,
        mesh=mesh,
        in_specs=placed,
        out_specs=(P("dp", "sx", "sy", None), P(), P()),
        check_vma=False,
    )
```

profile of v0, /device:TPU:0, one launch (start us, length us, event | category | flops | bytes accessed | tf_op | source)
XLA Modules:
  0.0 222.1 jit_solution(9865173924206717439)
XLA Ops:
  7.2 0.8 convert_multiply_fusion
  8.1 0.3 broadcast_in_dim.22
  8.4 0.5 mul.194
  9.1 0.3 convert_reduce_fusion
  9.4 1.3 collective-permute-start.1
  10.7 4.9 %collective-permute-start = (bf16[1,1,4,4096]{3,2,1,0:T(4,128)(2,1)S(1)}, bf16[1,1,4,4096]{3,2,1,0:T(4,128)(2,1)S(1)}, u32[]{:S(2)}, u32[]{:S(2)}) collective-permute-start(bf16[1,1,4,4096]{3,2,1,0:T(4,128)(2,1)S(1)} %get-tuple-element.35), channel_id=1, source_target_pairs={{0,4},{1,5},{2,6},{3,7},{8,12},{9,13},{10,14},{11,15},{16,20},{17,... | collective-permute-start | bytes 98312 | tf_op jit(solution)/shard_map/ppermute | solution.py:14
  15.6 1.3 collective-permute-start.4
  16.9 1.3 collective-permute-start.5
  18.2 0.5 select_n.102
  18.8 0.3 multiply_convert_fusion
  19.1 42.7 %psum.15 = f32[1,128]{1,0:T(1,128)S(1)} all-reduce(f32[1,128]{1,0:T(1,128)S(1)} %bitcast.528), channel_id=1, replica_groups=mesh['dp'=4,'sx'=2,'sy'=4] {'dp','sx','sy'}, use_global_device_ids=true, to_apply=%region_3.4 | all-reduce | flops 128 | bytes 1024 | tf_op jit(solution)/shard_map/psum | solution.py:81
  61.8 0.5 multiply_bitcast_fusion
  62.6 1.3 collective-permute-start.7
  63.9 4.6 %collective-permute-start.6 = (bf16[1,10,1,2048]{3,2,1,0:T(2,128)(2,1)S(1)}, bf16[1,10,1,2048]{3,2,1,0:T(2,128)(2,1)S(1)}, u32[]{:S(2)}, u32[]{:S(2)}) collective-permute-start(bf16[1,10,1,2048]{3,2,1,0:T(2,128)(2,1)S(1)} %get-tuple-element.37), channel_id=1, source_target_pairs={{0,1},{1,2},{2,3},{4,5},{5,6},{6,7},{8,9},{9,10},{10,11},{12,13},{... | collective-permute-start | bytes 122888 | tf_op jit(solution)/shard_map/ppermute | solution.py:14
  68.5 0.2 pad_maximum_fusion.1
  68.7 0.3 fusion.138
  69.1 1.3 collective-permute-start.3
  70.4 4.7 %collective-permute-start.2 = (bf16[1,10,1,4096]{3,2,1,0:T(2,128)(2,1)S(1)}, bf16[1,10,1,4096]{3,2,1,0:T(2,128)(2,1)S(1)}, u32[]{:S(2)}, u32[]{:S(2)}) collective-permute-start(bf16[1,10,1,4096]{3,2,1,0:T(2,128)(2,1)S(1)} %get-tuple-element.32), channel_id=1, source_target_pairs={{0,1},{1,2},{2,3},{4,5},{5,6},{6,7},{8,9},{9,10},{10,11},{12,13},{... | collective-permute-start | bytes 245768 | tf_op jit(solution)/shard_map/ppermute | solution.py:14
  75.1 0.3 pad_maximum_fusion.2
  75.4 0.5 reshape.527
  75.9 0.2 fusion.27
  76.4 0.2 fusion.25
  76.6 0.2 fusion.24
  77.1 0.2 fusion.22
  77.4 0.2 fusion.21
  77.9 0.2 fusion.19
  78.1 0.2 fusion.18
  78.4 0.2 fusion.17
  78.6 0.2 fusion.16
  78.9 0.2 fusion.15
  79.4 0.2 fusion.13
  79.6 0.2 fusion.12
  80.1 0.2 fusion.10
  80.3 0.2 fusion.9
  80.8 0.2 fusion.7
  81.1 0.2 fusion.6
  81.3 0.2 fusion.5
  81.6 0.2 fusion.4
  81.8 0.2 fusion.3
  82.3 0.2 fusion.1
  82.6 0.9 copy-done
  83.5 0.5 pad_maximum_fusion
  84.1 0.6 reshape.498
  84.7 0.4 fusion.137
  85.1 1.4 pad_slice_fusion.18
  92.5 0.9 reshape.526
  93.4 119.7 %all-reduce.4.cloned.1.call-done = f32[1728,128]{1,0:T(8,128)} async-done(((f32[1728,128]{1,0:T(8,128)}), f32[1728,128]{1,0:T(8,128)}) %all-reduce.4.cloned.1.call-update) | async-done | bytes 884752 | tf_op jit(solution)/shard_map/psum | solution.py:81
  213.1 2.1 broadcast_multiply_fusion
  (62 shorter events, 8.0 us)
Async XLA Ops:
  7.2 205.9 %all-reduce.4.cloned.1.call-start = ((), (), s32[]{:S(2)}) async-start(), calls=%async_computation | async-start | bytes 1769472 | tf_op jit(solution)/shard_map/psum | solution.py:81
  8.1 1.0 copy-start.2
  9.1 6.5 %copy-start.3 = (bf16[1,8,4,2048]{3,2,1,0:T(4,128)(2,1)S(1)}, bf16[1,8,4,2048]{3,2,1,0:T(4,128)(2,1)}, u32[]{:S(2)}) copy-start(bf16[1,8,4,2048]{3,2,1,0:T(4,128)(2,1)} %param.4) | copy-start | bytes 393220
  9.4 59.1 %collective-permute-start.1 = (bf16[1,1,4,4096]{3,2,1,0:T(4,128)(2,1)S(1)}, bf16[1,1,4,4096]{3,2,1,0:T(4,128)(2,1)S(1)}, u32[]{:S(2)}, u32[]{:S(2)}) collective-permute-start(bf16[1,1,4,4096]{3,2,1,0:T(4,128)(2,1)S(1)} %get-tuple-element.36), channel_id=1, source_target_pairs={{4,0},{5,1},{6,2},{7,3},{12,8},{13,9},{14,10},{15,11},{20,16},{21,... | collective-permute-start | bytes 98312 | tf_op jit(solution)/shard_map/ppermute | solution.py:17
  10.7 57.8 %collective-permute-start = (bf16[1,1,4,4096]{3,2,1,0:T(4,128)(2,1)S(1)}, bf16[1,1,4,4096]{3,2,1,0:T(4,128)(2,1)S(1)}, u32[]{:S(2)}, u32[]{:S(2)}) collective-permute-start(bf16[1,1,4,4096]{3,2,1,0:T(4,128)(2,1)S(1)} %get-tuple-element.35), channel_id=1, source_target_pairs={{0,4},{1,5},{2,6},{3,7},{8,12},{9,13},{10,14},{11,15},{16,20},{17,... | collective-permute-start | bytes 98312 | tf_op jit(solution)/shard_map/ppermute | solution.py:14
  15.6 46.7 %collective-permute-start.4 = (bf16[1,1,4,2048]{3,2,1,0:T(4,128)(2,1)S(1)}, bf16[1,1,4,2048]{3,2,1,0:T(4,128)(2,1)S(1)}, u32[]{:S(2)}, u32[]{:S(2)}) collective-permute-start(bf16[1,1,4,2048]{3,2,1,0:T(4,128)(2,1)S(1)} %get-tuple-element.40), channel_id=1, source_target_pairs={{0,4},{1,5},{2,6},{3,7},{8,12},{9,13},{10,14},{11,15},{16,20},{17,... | collective-permute-start | bytes 49160 | tf_op jit(solution)/shard_map/ppermute | solution.py:14
  16.9 45.5 %collective-permute-start.5 = (bf16[1,1,4,2048]{3,2,1,0:T(4,128)(2,1)S(1)}, bf16[1,1,4,2048]{3,2,1,0:T(4,128)(2,1)S(1)}, u32[]{:S(2)}, u32[]{:S(2)}) collective-permute-start(bf16[1,1,4,2048]{3,2,1,0:T(4,128)(2,1)S(1)} %get-tuple-element.39), channel_id=1, source_target_pairs={{4,0},{5,1},{6,2},{7,3},{12,8},{13,9},{14,10},{15,11},{20,16},{21,... | collective-permute-start | bytes 49160 | tf_op jit(solution)/shard_map/ppermute | solution.py:17
  62.6 12.5 %collective-permute-start.7 = (bf16[1,10,1,2048]{3,2,1,0:T(2,128)(2,1)S(1)}, bf16[1,10,1,2048]{3,2,1,0:T(2,128)(2,1)S(1)}, u32[]{:S(2)}, u32[]{:S(2)}) collective-permute-start(bf16[1,10,1,2048]{3,2,1,0:T(2,128)(2,1)S(1)} %get-tuple-element.38), channel_id=1, source_target_pairs={{1,0},{2,1},{3,2},{5,4},{6,5},{7,6},{9,8},{10,9},{11,10},{13,12},{... | collective-permute-start | bytes 122888 | tf_op jit(solution)/shard_map/ppermute | solution.py:17
  63.9 11.2 %collective-permute-start.6 = (bf16[1,10,1,2048]{3,2,1,0:T(2,128)(2,1)S(1)}, bf16[1,10,1,2048]{3,2,1,0:T(2,128)(2,1)S(1)}, u32[]{:S(2)}, u32[]{:S(2)}) collective-permute-start(bf16[1,10,1,2048]{3,2,1,0:T(2,128)(2,1)S(1)} %get-tuple-element.37), channel_id=1, source_target_pairs={{0,1},{1,2},{2,3},{4,5},{5,6},{6,7},{8,9},{9,10},{10,11},{12,13},{... | collective-permute-start | bytes 122888 | tf_op jit(solution)/shard_map/ppermute | solution.py:14
  69.1 14.5 %collective-permute-start.3 = (bf16[1,10,1,4096]{3,2,1,0:T(2,128)(2,1)S(1)}, bf16[1,10,1,4096]{3,2,1,0:T(2,128)(2,1)S(1)}, u32[]{:S(2)}, u32[]{:S(2)}) collective-permute-start(bf16[1,10,1,4096]{3,2,1,0:T(2,128)(2,1)S(1)} %get-tuple-element.33), channel_id=1, source_target_pairs={{1,0},{2,1},{3,2},{5,4},{6,5},{7,6},{9,8},{10,9},{11,10},{13,12},{... | collective-permute-start | bytes 245768 | tf_op jit(solution)/shard_map/ppermute | solution.py:17
  70.4 13.2 %collective-permute-start.2 = (bf16[1,10,1,4096]{3,2,1,0:T(2,128)(2,1)S(1)}, bf16[1,10,1,4096]{3,2,1,0:T(2,128)(2,1)S(1)}, u32[]{:S(2)}, u32[]{:S(2)}) collective-permute-start(bf16[1,10,1,4096]{3,2,1,0:T(2,128)(2,1)S(1)} %get-tuple-element.32), channel_id=1, source_target_pairs={{0,1},{1,2},{2,3},{4,5},{5,6},{6,7},{8,9},{9,10},{10,11},{12,13},{... | collective-permute-start | bytes 245768 | tf_op jit(solution)/shard_map/ppermute | solution.py:14
  82.6 0.9 copy-start
  85.1 1.5 copy-start.1
Sparse Core Ops, SparseCore 0:
  83.6 129.4 all-reduce.3
where the time goes:
time: 223 us; the launch traced here: 222 us
  waiting for transfers between devices  120 us (54%)
  blocking collectives  42.7 us (19%)
  starting transfers between devices  20.7 us (9%)
  between operations  14.7 us (7%)
  matrix products  12.1 us (5%)
  local copies, waits for them, and re-layouts  6.97 us (3%)
  other arithmetic  5.1 us (2%)
    psum x1, waiting for transfers between devices, on_device(): lax.psum((weight_sum, bias_sum), ('dp', 'sx', 'sy'))  120 us
    psum x1, blocking collectives, on_device(): lax.psum((weight_sum, bias_sum), ('dp', 'sx', 'sy'))  42.7 us
    ppermute x4, starting transfers between devices, extended(): lax.ppermute(lax.slice_in_dim(block, block.shape[dim] - width, None, axis...  15.5 us
    dot_general x27, matrix products, on_device(): lax.dot_general(act_moved, grad_flat, contract, preferred_element_type=jn...  6.5 us
    dot_general x27, matrix products, on_device(): lax.dot_general(moved, weights[index], backward, preferred_element_type=j...  5.61 us
    ppermute x4, starting transfers between devices, extended(): lax.ppermute(lax.slice_in_dim(block, 0, width, axis=dim), axis, backward)  5.17 us
  transfers between devices with their start and end apart: 9, of which 1 were waited for; matrix products, arithmetic and copies ran while one was open for 9% of the time, Pallas kernels for 0%

commit v1 on v0

v1 whole, which is shorter than its diff:
```python
import functools

import jax
import jax.numpy as jnp
from jax import lax
from jax.experimental import pallas as pl
from jax.experimental.pallas import tpu as pltpu
from jax.sharding import PartitionSpec as P

MESH = pl.DeviceIdType.MESH
AXES = ("dp", "sx", "sy")
ROWS = 8


def stage_kinds(sizes):
    count = dict(zip(AXES, sizes))
    kinds = []
    if count["dp"] % 2 == 0:
        kinds.append(("core", 2))
        kinds.append(("chip", count["dp"] // 2))
    else:
        kinds.append(("dp", count["dp"]))
    kinds.append(("sx", count["sx"]))
    kinds.append(("sy", count["sy"]))
    return [kind for kind in kinds if kind[1] > 1]


def plan_parts(units, sizes):
    kinds = stage_kinds(sizes)
    devices = sizes[0] * sizes[1] * sizes[2]
    granules = -(-units // devices)
    names = [kind[0] for kind in kinds]
    if granules == 1 or "chip" not in names or "sx" not in names:
        return [(0, granules * devices, kinds)]
    first = -(-granules // 2)
    chip, side = names.index("chip"), names.index("sx")
    other = list(kinds)
    other[chip], other[side] = kinds[side], kinds[chip]
    return [
        (0, first * devices, kinds),
        (first * devices, (granules - first) * devices, other),
    ]


def chunks_of(part):
    sizes, length = [], part[1]
    for _, count in part[2]:
        length //= count
        sizes.append(length)
    return sizes


def place():
    return tuple(lax.axis_index(axis) for axis in AXES)


def member(kind, here):
    d, x, y = here
    return {"core": d % 2, "chip": d // 2, "dp": d, "sx": x, "sy": y}[kind]


def peer(kind, here, index):
    d, x, y = here
    if kind == "core":
        return (d - d % 2 + index, x, y)
    if kind == "chip":
        return (2 * index + d % 2, x, y)
    if kind == "dp":
        return (index, x, y)
    if kind == "sx":
        return (d, index, y)
    return (d, x, index)


def body(sizes, parts, samples, gate_ref, act_ref, weights_ref, grad_ref, total_ref, *scratch):
    count_parts = len(parts)
    gcat, acc, halo_x, halo_y, corner, input_acc = scratch[:6]
    landing = scratch[6 : 6 + count_parts]
    halo_send, halo_recv = scratch[6 + count_parts : 8 + count_parts]
    sems = scratch[8 + count_parts :]
    cells_x, cells_y, cells_z, chan_out = gate_ref.shape
    offsets, chan_in, _ = weights_ref.shape
    cells = cells_x * cells_y * cells_z
    units = chan_in // ROWS
    bias_unit = offsets * units
    here = place()
    d, x, y = here
    kinds = stage_kinds(sizes)

    barrier = pltpu.get_barrier_semaphore()
    greeted = 0
    for kind, count in kinds:
        for turn in range(1, count):
            target = peer(kind, here, (member(kind, here) + turn) % count)
            pl.semaphore_signal(barrier, inc=1, device_id=target, device_id_type=MESH)
            greeted += 1
    diagonals = [(dx, dy) for dx in (-1, 1) for dy in (-1, 1)]

    def inside(dx, dy):
        ok = None
        for coord, step, size in ((x, dx, sizes[1]), (y, dy, sizes[2])):
            if step == -1:
                term = coord > 0
            elif step == 1:
                term = coord < size - 1
            else:
                continue
            ok = term if ok is None else jnp.logical_and(ok, term)
        return ok

    for dx, dy in diagonals:
        @pl.when(inside(dx, dy))
        def _():
            pl.semaphore_signal(
                barrier, inc=1, device_id=(d, x + dx, y + dy), device_id_type=MESH
            )
    for dx, dy in diagonals:
        greeted = greeted + jnp.where(inside(dx, dy), 1, 0)
    pl.semaphore_wait(barrier, greeted)

    def side(step):
        return 0 if step == -1 else 1

    def edge(step, size):
        return 0 if step == -1 else size - 1

    def halo_copy(dx, dy):
        if dy == 0:
            src = gate_ref.at[edge(dx, cells_x)]
            dst = halo_x.at[side(-dx)]
            slot = side(dx)
            back = side(-dx)
        elif dx == 0:
            src = gate_ref.at[:, edge(dy, cells_y)]
            dst = halo_y.at[side(-dy)]
            slot = 2 + side(dy)
            back = 2 + side(-dy)
        else:
            src = gate_ref.at[edge(dx, cells_x), edge(dy, cells_y)]
            dst = corner.at[2 * side(-dx) + side(-dy)]
            slot = 4 + 2 * side(dx) + side(dy)
            back = 4 + 2 * side(-dx) + side(-dy)
        return pltpu.make_async_remote_copy(
            src_ref=src,
            dst_ref=dst,
            send_sem=halo_send.at[slot],
            recv_sem=halo_recv.at[back],
            device_id=(d, x + dx, y + dy),
            device_id_type=MESH,
        )

    ways = [(0, -1), (0, 1), (-1, 0), (1, 0)] + diagonals
    for dx, dy in ways:
        @pl.when(inside(dx, dy))
        def _():
            halo_copy(dx, dy).start()

    def widen(block):
        shape = block.shape
        wide = block.astype(jnp.float32).reshape(-1, cells_z, chan_out)
        depth = lax.broadcasted_iota(jnp.int32, wide.shape, 1)
        low = jnp.where(depth == cells_z - 1, 0.0, pltpu.roll(wide, cells_z - 1, 1))
        high = jnp.where(depth == 0, 0.0, pltpu.roll(wide, 1, 1))
        return jnp.concatenate(
            [low.astype(jnp.bfloat16), block.reshape(wide.shape), high.astype(jnp.bfloat16)],
            axis=-1,
        ).reshape(shape[:-1] + (3 * chan_out,))

    bias = jnp.zeros((ROWS, chan_out), jnp.float32)
    for row in range(cells_x):
        block = gate_ref[row]
        gcat[1 + row, pl.ds(1, cells_y)] = widen(block)
        bias = bias + jnp.sum(block.astype(jnp.float32).reshape(-1, ROWS, chan_out), axis=0)
    bias = jnp.sum(bias, axis=0, keepdims=True)
    top = lax.broadcasted_iota(jnp.int32, (ROWS, chan_out), 0) == 0
    acc[bias_unit] = jnp.where(top, jnp.broadcast_to(bias, (ROWS, chan_out)), 0.0)
    spare = acc.shape[0] - bias_unit - 1
    if spare:
        acc[pl.ds(bias_unit + 1, spare)] = jnp.zeros((spare, ROWS, chan_out), jnp.float32)

    for dx, dy in ways:
        ex = slice(1, 1 + cells_x) if dx == 0 else (0 if dx == -1 else cells_x + 1)
        ey = slice(1, 1 + cells_y) if dy == 0 else (0 if dy == -1 else cells_y + 1)

        @pl.when(inside(dx, dy))
        def _():
            halo_copy(-dx, -dy).wait_recv()
            if dy == 0:
                gcat[ex, ey] = widen(halo_x[side(dx)])
            elif dx == 0:
                gcat[ex, ey] = widen(halo_y[side(dy)])
            else:
                gcat[ex, ey] = widen(corner[2 * side(dx) + side(dy)])

        @pl.when(jnp.logical_not(inside(dx, dy)))
        def _():
            ref = gcat.at[ex, ey]
            ref[...] = jnp.zeros(ref.shape, jnp.bfloat16)

    started = []
    chunk_sizes = [chunks_of(part) for part in parts]
    starts = [[jnp.int32(part[0])] for part in parts]

    def slot_of(p, stage, turn):
        base = sum(count - 1 for _, count in parts[p][2][:stage])
        return base + turn - 1

    def row_of(p, stage, turn):
        base = 0
        for earlier in range(stage):
            base += (parts[p][2][earlier][1] - 1) * chunk_sizes[p][earlier]
        return base + (turn - 1) * chunk_sizes[p][stage]

    pending = [None] * count_parts

    def send_reduce(p, stage):
        kind, count = parts[p][2][stage]
        chunk = chunk_sizes[p][stage]
        me = member(kind, here)
        copies = []
        for turn in range(1, count):
            index = (me + turn) % count
            slot = slot_of(p, stage, turn)
            copy = pltpu.make_async_remote_copy(
                src_ref=acc.at[pl.ds(starts[p][-1] + index * chunk, chunk)],
                dst_ref=landing[p].at[pl.ds(row_of(p, stage, turn), chunk)],
                send_sem=sems[2 * p].at[0, slot],
                recv_sem=sems[2 * p + 1].at[0, slot],
                device_id=peer(kind, here, index),
                device_id_type=MESH,
            )
            copy.start()
            copies.append(copy)
            started.append(copy)
        pending[p] = copies

    def take_reduce(p, stage):
        kind, count = parts[p][2][stage]
        chunk = chunk_sizes[p][stage]
        own = starts[p][-1] + member(kind, here) * chunk
        starts[p].append(own)
        value = acc[pl.ds(own, chunk)]
        for turn in range(1, count):
            pending[p][turn - 1].wait_recv()
            value = value + landing[p][pl.ds(row_of(p, stage, turn), chunk)]
        acc[pl.ds(own, chunk)] = value

    def round_shard(p):
        own, chunk = starts[p][-1], chunk_sizes[p][-1]
        value = acc[pl.ds(own, chunk)] * (1.0 / (samples * sizes[0]))
        high = value.astype(jnp.bfloat16).astype(jnp.float32)
        rest = pltpu.roll(value - high, 1, 1)
        unit = own + lax.broadcasted_iota(jnp.int32, value.shape, 0)
        row = lax.broadcasted_iota(jnp.int32, value.shape, 1)
        kept = jnp.where(jnp.logical_and(unit == bias_unit, row == 1), rest, high)
        total_ref[pl.ds(own, chunk)] = kept.astype(jnp.bfloat16)

    def send_gather(p, stage):
        kind, count = parts[p][2][stage]
        chunk = chunk_sizes[p][stage]
        own = starts[p][stage + 1]
        me = member(kind, here)
        copies = []
        for turn in range(1, count):
            slot = slot_of(p, stage, turn)
            copy = pltpu.make_async_remote_copy(
                src_ref=total_ref.at[pl.ds(own, chunk)],
                dst_ref=total_ref.at[pl.ds(own, chunk)],
                send_sem=sems[2 * p].at[1, slot],
                recv_sem=sems[2 * p + 1].at[1, slot],
                device_id=peer(kind, here, (me + turn) % count),
                device_id_type=MESH,
            )
            copy.start()
            copies.append(copy)
            started.append(copy)
        pending[p] = copies

    ready = 0
    for a in (-1, 0, 1):
        for b in (-1, 0, 1):
            first = 9 * (a + 1) + 3 * (b + 1)
            moved = gcat[pl.ds(1 - a, cells_x), pl.ds(1 - b, cells_y)]
            term = jnp.dot(
                act_ref[...],
                moved.reshape(cells, 3 * chan_out),
                preferred_element_type=jnp.float32,
            )
            for c in range(3):
                acc[pl.ds((first + c) * units, units)] = term[
                    :, c * chan_out : (c + 1) * chan_out
                ].reshape(units, ROWS, chan_out)
            done = (first + 3) * units
            while ready < count_parts - 1 and parts[ready][0] + parts[ready][1] <= done:
                send_reduce(ready, 0)
                ready += 1
    while ready < count_parts:
        send_reduce(ready, 0)
        ready += 1

    def input_piece(a):
        total = None
        for b in (-1, 0, 1):
            first = 9 * (a + 1) + 3 * (b + 1)
            moved = gcat[pl.ds(1 - a, cells_x), pl.ds(1 - b, cells_y)]
            wide = jnp.concatenate([weights_ref[first + c] for c in range(3)], axis=1)
            term = lax.dot_general(
                moved.reshape(cells, 3 * chan_out),
                wide,
                (((1,), (1,)), ((), ())),
                preferred_element_type=jnp.float32,
            )
            total = term if total is None else total + term
        if a == -1:
            input_acc[...] = total
        elif a == 0:
            input_acc[...] += total
        else:
            grad_ref[...] = (input_acc[...] + total).astype(jnp.bfloat16)

    pieces = [-1, 0, 1]
    stages = len(kinds)
    for stage in range(stages):
        if pieces:
            input_piece(pieces.pop(0))
        for p in range(count_parts):
            take_reduce(p, stage)
            if stage + 1 < stages:
                send_reduce(p, stage + 1)
            else:
                round_shard(p)
                send_gather(p, stage)
    for a in pieces:
        input_piece(a)
    for stage in reversed(range(stages)):
        for p in range(count_parts):
            for copy in pending[p]:
                copy.wait_recv()
            if stage:
                send_gather(p, stage - 1)
    for copy in started:
        copy.wait_send()
    for dx, dy in ways:
        @pl.when(inside(dx, dy))
        def _():
            halo_copy(dx, dy).wait_send()


def fused(gate, acts, weights, samples, sizes):
    cells_x, cells_y, cells_z, chan_out = gate.shape
    offsets, chan_in, _ = weights.shape
    needed = offsets * chan_in // ROWS + 1
    parts = plan_parts(needed, sizes)
    units = sum(part[1] for part in parts)
    scratch = [
        pltpu.VMEM((cells_x + 2, cells_y + 2, cells_z, 3 * chan_out), jnp.bfloat16),
        pltpu.VMEM((units, ROWS, chan_out), jnp.float32),
        pltpu.VMEM((2, cells_y, cells_z, chan_out), jnp.bfloat16),
        pltpu.VMEM((2, cells_x, cells_z, chan_out), jnp.bfloat16),
        pltpu.VMEM((4, cells_z, chan_out), jnp.bfloat16),
        pltpu.VMEM((acts.shape[1], chan_in), jnp.float32),
    ]
    for part in parts:
        rows = sum(
            (count - 1) * chunk for (_, count), chunk in zip(part[2], chunks_of(part))
        )
        scratch.append(pltpu.VMEM((rows, ROWS, chan_out), jnp.float32))
    scratch += [pltpu.SemaphoreType.DMA((8,)), pltpu.SemaphoreType.DMA((8,))]
    for part in parts:
        slots = sum(count - 1 for _, count in part[2])
        scratch += [pltpu.SemaphoreType.DMA((2, slots)), pltpu.SemaphoreType.DMA((2, slots))]
    return pl.pallas_call(
        functools.partial(body, sizes, parts, samples),
        out_shape=(
            jax.ShapeDtypeStruct((acts.shape[1], chan_in), jnp.bfloat16),
            jax.ShapeDtypeStruct((units, ROWS, chan_out), jnp.bfloat16),
        ),
        in_specs=[pl.BlockSpec(memory_space=pltpu.VMEM)] * 3,
        out_specs=(pl.BlockSpec(memory_space=pltpu.VMEM),) * 2,
        scratch_shapes=scratch,
        compiler_params=pltpu.CompilerParams(
            collective_id=0, has_side_effects=True, vmem_limit_bytes=48 * 1024 * 1024
        ),
    )(gate, acts, weights)


def on_device(sizes, activations, preact, pooled_grad, weights):
    samples, cells_x, cells_y, flat_in = activations.shape
    offsets, chan_in, chan_out = weights.shape
    cells_z = flat_in // chan_in
    rows_x = samples * cells_x
    upper = pooled_grad.reshape(rows_x // 2, cells_y // 2, cells_z // 2, chan_out)
    grad_act = (
        jnp.repeat(jnp.repeat(jnp.repeat(upper, 2, 0), 2, 1), 2, 2).astype(jnp.float32) * 0.125
    )
    slope = jnp.where(
        preact.reshape(rows_x, cells_y, cells_z, chan_out) > 0, 1.0, 0.3
    ).astype(jnp.float32)
    gate = (grad_act * slope).astype(jnp.bfloat16)
    acts = activations.reshape(-1, chan_in).T
    grad, total = fused(gate, acts, weights, samples, sizes)
    input_grad = grad.reshape(activations.shape)
    unit = offsets * chan_in // ROWS
    weight_grad = total[:unit].astype(jnp.float32).reshape(offsets, chan_in, chan_out)
    bias = total[unit].astype(jnp.float32)
    return (input_grad, weight_grad, bias[0] + bias[1])


def solution(mesh):
    sizes = tuple(mesh.shape[axis] for axis in AXES)
    placed = (P("dp", "sx", "sy", None), P("dp", "sx", "sy", None), P("dp", "sx", "sy", None), P())
    return jax.shard_map(
        functools.partial(on_device, sizes),
        mesh=mesh,
        in_specs=placed,
        out_specs=(P("dp", "sx", "sy", None), P(), P()),
        check_vma=False,
    )
```

time: 223 us -> 43.7 us (0.20)
  waiting for transfers between devices: 120 us -> 0 us
  blocking collectives: 42.7 us -> 0 us
  Pallas kernels: 0 us -> 35.8 us
  starting transfers between devices: 20.7 us -> 0 us
  between operations: 14.7 us -> 0.74 us
  matrix products: 12.1 us -> 0 us
  local copies, waits for them, and re-layouts: 6.97 us -> 4.33 us
  other arithmetic: 5.1 us -> 2.54 us
    psum x1 -> x0, waiting for transfers between devices: 120 us -> none  [on_device(): lax.psum((weight_sum, bias_sum), ('dp', 'sx', 'sy'))]
    psum x1 -> x0, blocking collectives: 42.7 us -> none  [on_device(): lax.psum((weight_sum, bias_sum), ('dp', 'sx', 'sy'))]
    pallas_call x0 -> x1, Pallas kernels: none -> 35.8 us  [fused(): pl.pallas_call(functools.partial(body, sizes, parts, samples), out_shape=...]
    ppermute x8 -> x0, starting transfers between devices: 20.6 us -> none  [the longest x4 15.5 us: extended(): lax.ppermute(lax.slice_in_dim(block, block.shape[dim] - width, None, axis...]
    dot_general x54 -> x0, matrix products: 12.1 us -> none  [the longest x27 6.5 us: on_device(): lax.dot_general(act_moved, grad_flat, contract, preferred_element_type=jn...]
    div x2 -> x0, other arithmetic: 2.65 us -> none  [the longest x1 2.14 us: on_device(): weight_grad = (weight_total / total_samples).reshape(27, chan_in, chan_out)]
    slice x6 -> x1, local copies, waits for them, and re-layouts: 2.3 us -> 0.03 us  [on_device(): total[:unit].astype(jnp.float32).reshape(offsets, chan_in, chan_out)]
  transfers between devices with their start and end apart: 9 -> 0, of which waited for: 1 -> 0; matrix products, arithmetic and copies ran while one was open for 9% -> 0% of each run, Pallas kernels for 0% -> 0%
where the time goes in v1:
time: 43.7 us; the launch traced here: 43.4 us
  Pallas kernels  35.8 us (82%)
  local copies, waits for them, and re-layouts  4.33 us (10%)
  other arithmetic  2.54 us (6%)
  between operations  0.74 us (2%)
    pallas_call x1, Pallas kernels, fused(): pl.pallas_call(functools.partial(body, sizes, parts, samples), out_shape=...  35.8 us
    unnamed x6, local copies, waits for them, and re-layouts  2.35 us
    reshape x1, other arithmetic, on_device(): total[:unit].astype(jnp.float32).reshape(offsets, chan_in, chan_out)  1.01 us

profile of v1, /device:TPU:0, one launch (start us, length us, event | category | flops | bytes accessed | tf_op | source)
XLA Modules:
  0.0 43.4 jit_solution(15198808199849874645)
XLA Ops:
  0.6 0.8 %convert_multiply_fusion = f32[1,4,2,2048]{3,2,1,0:T(2,128)S(1)} fusion(bf16[1,4,2,2048]{3,2,1,0:T(2,128)(2,1)} %param.6), kind=kLoop, calls=%fused_computation.3 | loop fusion | flops 32768 | bytes 98304 | tf_op jit(solution)/shard_map/mul | solution.py:394
  1.4 0.1 reshape.53
  1.5 0.0 copy-start.2
  1.5 0.3 broadcast_in_dim.19
  1.8 0.6 %copy-done.2 = bf16[1,8,4,2048]{3,2,1,0:T(4,128)(2,1)S(1)} copy-done((bf16[1,8,4,2048]{3,2,1,0:T(4,128)(2,1)S(1)}, bf16[1,8,4,2048]{3,2,1,0:T(4,128)(2,1)}, u32[]{:S(2)}) %copy-start.2) | copy-done | bytes 131096
  2.4 0.3 reshape.45
  2.7 0.0 copy-start.1
  2.7 0.1 copy.7
  2.8 0.8 %copy-done.1 = bf16[1,8,4,4096]{3,2,1,0:T(4,128)(2,1)S(1)} copy-done((bf16[1,8,4,4096]{3,2,1,0:T(4,128)(2,1)S(1)}, bf16[1,8,4,4096]{3,2,1,0:T(4,128)(2,1)}, u32[]{:S(2)}) %copy-start.1) | copy-done | bytes 262168
  3.7 0.1 compare_select_fusion
  3.8 0.4 select_n.8
  4.2 0.0 copy-start
  4.2 0.1 multiply_convert_fusion.gate_ref
  4.3 0.9 %copy-done = bf16[27,64,128]{2,1,0:T(8,128)(2,1)S(1)} copy-done((bf16[27,64,128]{2,1,0:T(8,128)(2,1)S(1)}, bf16[27,64,128]{2,1,0:T(8,128)(2,1)}, u32[]{:S(2)}) %copy-start) | copy-done | bytes 442392
  5.2 35.8 %shard_map.67 = (bf16[1024,64]{1,0:T(8,128)(2,1)S(1)}, bf16[224,8,128]{2,1,0:T(8,128)(2,1)S(1)}) custom-call(bf16[8,4,32,128]{3,2,1,0:T(8,128)(2,1)S(1)} %multiply_convert_fusion.gate_ref, bf16[64,1024]{1,0:T(8,128)(2,1)S(1)} %bitcast.10, bf16[27,64,128]{2,1,0:T(8,128)(2,1)S(1)} %copy-done), custom_call_target="tpu_custom_call" | custom-call | tf_op jit(solution)/shard_map/pallas_call | solution.py:372
  41.0 0.9 %reshape.46 = bf16[1,8,4,2048]{3,2,1,0:T(4,128)(2,1)} reshape(bf16[1024,64]{1,0:T(8,128)(2,1)S(1)} %get-tuple-element.5) | data formatting | bytes 262144 | tf_op jit(solution)/shard_map/reshape | solution.py:402
  41.9 0.5 %add_bitcast_fusion = f32[128]{0:T(128)} fusion(f32[1,8,128]{2,1,0:T(8,128)S(1)} %slice_convert_fusion), kind=kLoop, calls=%fused_computation.5 | loop fusion | flops 128 | bytes 1536 | tf_op jit(solution)/shard_map/add | solution.py:406
  42.4 1.0 %bitcast_convert_fusion = f32[27,64,128]{2,1,0:T(8,128)} fusion(bf16[27,64,128]{2,1,0:T(8,128)(2,1)S(1)} %bitcast.12), kind=kLoop, calls=%fused_computation.2 | loop fusion | flops 221184 | bytes 1327104 | tf_op jit(solution)/shard_map/reshape | solution.py:404
  (4 shorter events, 0.1 us)
Async XLA Ops:
  1.5 0.9 %copy-start.2 = (bf16[1,8,4,2048]{3,2,1,0:T(4,128)(2,1)S(1)}, bf16[1,8,4,2048]{3,2,1,0:T(4,128)(2,1)}, u32[]{:S(2)}) copy-start(bf16[1,8,4,2048]{3,2,1,0:T(4,128)(2,1)} %param.4) | copy-start | bytes 393220
  2.7 1.0 %copy-start.1 = (bf16[1,8,4,4096]{3,2,1,0:T(4,128)(2,1)S(1)}, bf16[1,8,4,4096]{3,2,1,0:T(4,128)(2,1)}, u32[]{:S(2)}) copy-start(bf16[1,8,4,4096]{3,2,1,0:T(4,128)(2,1)} %param.5) | copy-start | bytes 786436
  4.2 1.0 %copy-start = (bf16[27,64,128]{2,1,0:T(8,128)(2,1)S(1)}, bf16[27,64,128]{2,1,0:T(8,128)(2,1)}, u32[]{:S(2)}) copy-start(bf16[27,64,128]{2,1,0:T(8,128)(2,1)} %weights_ref.1) | copy-start | bytes 1327108

commit v2 on v1

--- a/solution.py
+++ b/solution.py
@@ -1,4 +1,5 @@
 import functools
+import itertools
 
 import jax
 import jax.numpy as jnp
@@ -12,34 +13,40 @@
 ROWS = 8
 
 
-def stage_kinds(sizes):
-    count = dict(zip(AXES, sizes))
+FACTORS = ("core", "chip", "sx", "sy")
+GROUPS = (
+    (("core", "chip", "sx"), ("sy",)),
+    (("core", "sy"), ("chip", "sx")),
+)
+CODE = 2.0**36
+
+
+def stage_kinds(sizes, groups):
     kinds = []
-    if count["dp"] % 2 == 0:
-        kinds.append(("core", 2))
-        kinds.append(("chip", count["dp"] // 2))
-    else:
-        kinds.append(("dp", count["dp"]))
-    kinds.append(("sx", count["sx"]))
-    kinds.append(("sy", count["sy"]))
-    return [kind for kind in kinds if kind[1] > 1]
+    for group in groups:
+        count = 1
+        for name in group:
+            count *= span(name, sizes)
+        if count > 1:
+            kinds.append((group, count))
+    return kinds
+
+
+def span(name, sizes):
+    pair = 2 if sizes[0] % 2 == 0 else 1
+    return {"core": pair, "chip": sizes[0] // pair, "sx": sizes[1], "sy": sizes[2]}[name]
 
 
 def plan_parts(units, sizes):
-    kinds = stage_kinds(sizes)
     devices = sizes[0] * sizes[1] * sizes[2]
     granules = -(-units // devices)
-    names = [kind[0] for kind in kinds]
-    if granules == 1 or "chip" not in names or "sx" not in names:
-        return [(0, granules * devices, kinds)]
-    first = -(-granules // 2)
-    chip, side = names.index("chip"), names.index("sx")
-    other = list(kinds)
-    other[chip], other[side] = kinds[side], kinds[chip]
-    return [
-        (0, first * devices, kinds),
-        (first * devices, (granules - first) * devices, other),
-    ]
+    count = min(len(GROUPS), granules)
+    parts, first = [], 0
+    for index in range(count):
+        share = -(-(granules - first) // (count - index))
+        parts.append((first * devices, share * devices, stage_kinds(sizes, GROUPS[index])))
+        first += share
+    return parts
 
 
 def chunks_of(part):
@@ -54,46 +61,83 @@
     return tuple(lax.axis_index(axis) for axis in AXES)
 
 
-def member(kind, here):
+def split(sizes, here):
     d, x, y = here
-    return {"core": d % 2, "chip": d // 2, "dp": d, "sx": x, "sy": y}[kind]
-
-
-def peer(kind, here, index):
-    d, x, y = here
-    if kind == "core":
-        return (d - d % 2 + index, x, y)
-    if kind == "chip":
-        return (2 * index + d % 2, x, y)
-    if kind == "dp":
-        return (index, x, y)
-    if kind == "sx":
-        return (d, index, y)
-    return (d, x, index)
-
-
-def body(sizes, parts, samples, gate_ref, act_ref, weights_ref, grad_ref, total_ref, *scratch):
+    pair = span("core", sizes)
+    return {"core": d % pair, "chip": d // pair, "sx": x, "sy": y}
+
+
+def member(sizes, group, here):
+    values = split(sizes, here)
+    index = 0
+    for name in group:
+        index = index * span(name, sizes) + values[name]
+    return index
+
+
+def peer(sizes, group, here, index):
+    values = split(sizes, here)
+    for name in reversed(group):
+        values[name] = index % span(name, sizes)
+        index = index // span(name, sizes)
+    return (values["chip"] * span("core", sizes) + values["core"], values["sx"], values["sy"])
+
+
+def meetings(sizes, parts):
+    found = set()
+    for part in parts:
+        for group, _ in part[2]:
+            ranges = [
+                range(span(name, sizes)) if name in group else range(1) for name in FACTORS
+            ]
+            found.update(itertools.product(*ranges))
+    found.discard((0,) * len(FACTORS))
+    return sorted(found)
+
+
+def moved_by(sizes, here, moves):
+    values = split(sizes, here)
+    for name, move in zip(FACTORS, moves):
+        if move:
+            values[name] = (values[name] + move) % span(name, sizes)
+    return (values["chip"] * span("core", sizes) + values["core"], values["sx"], values["sy"])
+
+
+def encode(value):
+    scaled = value * CODE
+    return (scaled * jnp.abs(scaled)).astype(jnp.bfloat16)
+
+
+def decode(coded):
+    wide = coded.astype(jnp.float32)
+    root = jnp.sqrt(jnp.abs(wide)) * (1.0 / CODE)
+    return jnp.where(wide < 0, -root, root)
+
+
+def body(sizes, parts, samples, gate_ref, act_ref, weights_hbm, grad_ref, total_ref, *scratch):
     count_parts = len(parts)
-    gcat, acc, halo_x, halo_y, corner, input_acc = scratch[:6]
-    landing = scratch[6 : 6 + count_parts]
-    halo_send, halo_recv = scratch[6 + count_parts : 8 + count_parts]
-    sems = scratch[8 + count_parts :]
+    weights_ref = scratch[0]
+    gcat, acc, halo_x, halo_y, corner, input_acc = scratch[1:7]
+    landing = scratch[7 : 7 + count_parts]
+    leaving = scratch[7 + count_parts : 7 + 2 * count_parts]
+    halo_send, halo_recv, weight_sem = scratch[7 + 2 * count_parts : 10 + 2 * count_parts]
+    sems = scratch[10 + 2 * count_parts :]
+    weight_copy = pltpu.make_async_copy(weights_hbm, weights_ref, weight_sem)
+    weight_copy.start()
     cells_x, cells_y, cells_z, chan_out = gate_ref.shape
-    offsets, chan_in, _ = weights_ref.shape
+    offsets, chan_in, _ = weights_hbm.shape
     cells = cells_x * cells_y * cells_z
     units = chan_in // ROWS
     bias_unit = offsets * units
     here = place()
     d, x, y = here
-    kinds = stage_kinds(sizes)
 
     barrier = pltpu.get_barrier_semaphore()
     greeted = 0
-    for kind, count in kinds:
-        for turn in range(1, count):
-            target = peer(kind, here, (member(kind, here) + turn) % count)
-            pl.semaphore_signal(barrier, inc=1, device_id=target, device_id_type=MESH)
-            greeted += 1
+    for moves in meetings(sizes, parts):
+        target = moved_by(sizes, here, moves)
+        pl.semaphore_signal(barrier, inc=1, device_id=target, device_id_type=MESH)
+        greeted += 1
     diagonals = [(dx, dy) for dx in (-1, 1) for dy in (-1, 1)]
 
     def inside(dx, dy):
@@ -216,17 +260,19 @@
     def send_reduce(p, stage):
         kind, count = parts[p][2][stage]
         chunk = chunk_sizes[p][stage]
-        me = member(kind, here)
+        me = member(sizes, kind, here)
         copies = []
         for turn in range(1, count):
             index = (me + turn) % count
             slot = slot_of(p, stage, turn)
+            rows = pl.ds(row_of(p, stage, turn), chunk)
+            leaving[p][rows] = encode(acc[pl.ds(starts[p][-1] + index * chunk, chunk)])
             copy = pltpu.make_async_remote_copy(
-                src_ref=acc.at[pl.ds(starts[p][-1] + index * chunk, chunk)],
-                dst_ref=landing[p].at[pl.ds(row_of(p, stage, turn), chunk)],
+                src_ref=leaving[p].at[rows],
+                dst_ref=landing[p].at[rows],
                 send_sem=sems[2 * p].at[0, slot],
                 recv_sem=sems[2 * p + 1].at[0, slot],
-                device_id=peer(kind, here, index),
+                device_id=peer(sizes, kind, here, index),
                 device_id_type=MESH,
             )
             copy.start()
@@ -237,29 +283,29 @@
     def take_reduce(p, stage):
         kind, count = parts[p][2][stage]
         chunk = chunk_sizes[p][stage]
-        own = starts[p][-1] + member(kind, here) * chunk
+        own = starts[p][-1] + member(sizes, kind, here) * chunk
         starts[p].append(own)
         value = acc[pl.ds(own, chunk)]
         for turn in range(1, count):
             pending[p][turn - 1].wait_recv()
-            value = value + landing[p][pl.ds(row_of(p, stage, turn), chunk)]
+            value = value + decode(landing[p][pl.ds(row_of(p, stage, turn), chunk)])
         acc[pl.ds(own, chunk)] = value
 
     def round_shard(p):
         own, chunk = starts[p][-1], chunk_sizes[p][-1]
         value = acc[pl.ds(own, chunk)] * (1.0 / (samples * sizes[0]))
-        high = value.astype(jnp.bfloat16).astype(jnp.float32)
-        rest = pltpu.roll(value - high, 1, 1)
+        coded = encode(value)
+        rest = pltpu.roll(value - decode(coded), 1, 1)
         unit = own + lax.broadcasted_iota(jnp.int32, value.shape, 0)
         row = lax.broadcasted_iota(jnp.int32, value.shape, 1)
-        kept = jnp.where(jnp.logical_and(unit == bias_unit, row == 1), rest, high)
-        total_ref[pl.ds(own, chunk)] = kept.astype(jnp.bfloat16)
+        is_rest = jnp.logical_and(unit == bias_unit, row == 1)
+        total_ref[pl.ds(own, chunk)] = encode(jnp.where(is_rest, rest, value))
 
     def send_gather(p, stage):
         kind, count = parts[p][2][stage]
         chunk = chunk_sizes[p][stage]
         own = starts[p][stage + 1]
-        me = member(kind, here)
+        me = member(sizes, kind, here)
         copies = []
         for turn in range(1, count):
             slot = slot_of(p, stage, turn)
@@ -268,7 +314,7 @@
                 dst_ref=total_ref.at[pl.ds(own, chunk)],
                 send_sem=sems[2 * p].at[1, slot],
                 recv_sem=sems[2 * p + 1].at[1, slot],
-                device_id=peer(kind, here, (me + turn) % count),
+                device_id=peer(sizes, kind, here, (me + turn) % count),
                 device_id_type=MESH,
             )
             copy.start()
@@ -318,8 +364,9 @@
         else:
             grad_ref[...] = (input_acc[...] + total).astype(jnp.bfloat16)
 
+    weight_copy.wait()
     pieces = [-1, 0, 1]
-    stages = len(kinds)
+    stages = max(len(part[2]) for part in parts)
     for stage in range(stages):
         if pieces:
             input_piece(pieces.pop(0))
@@ -353,6 +400,7 @@
     parts = plan_parts(needed, sizes)
     units = sum(part[1] for part in parts)
     scratch = [
+        pltpu.VMEM(weights.shape, weights.dtype),
         pltpu.VMEM((cells_x + 2, cells_y + 2, cells_z, 3 * chan_out), jnp.bfloat16),
         pltpu.VMEM((units, ROWS, chan_out), jnp.float32),
         pltpu.VMEM((2, cells_y, cells_z, chan_out), jnp.bfloat16),
@@ -360,12 +408,12 @@
         pltpu.VMEM((4, cells_z, chan_out), jnp.bfloat16),
         pltpu.VMEM((acts.shape[1], chan_in), jnp.float32),
     ]
-    for part in parts:
+    for part in parts + parts:
         rows = sum(
             (count - 1) * chunk for (_, count), chunk in zip(part[2], chunks_of(part))
         )
-        scratch.append(pltpu.VMEM((rows, ROWS, chan_out), jnp.float32))
-    scratch += [pltpu.SemaphoreType.DMA((8,)), pltpu.SemaphoreType.DMA((8,))]
+        scratch.append(pltpu.VMEM((rows, ROWS, chan_out), jnp.bfloat16))
+    scratch += [pltpu.SemaphoreType.DMA((8,)), pltpu.SemaphoreType.DMA((8,)), pltpu.SemaphoreType.DMA]
     for part in parts:
         slots = sum(count - 1 for _, count in part[2])
         scratch += [pltpu.SemaphoreType.DMA((2, slots)), pltpu.SemaphoreType.DMA((2, slots))]
@@ -375,7 +423,8 @@
             jax.ShapeDtypeStruct((acts.shape[1], chan_in), jnp.bfloat16),
             jax.ShapeDtypeStruct((units, ROWS, chan_out), jnp.bfloat16),
         ),
-        in_specs=[pl.BlockSpec(memory_space=pltpu.VMEM)] * 3,
+        in_specs=[pl.BlockSpec(memory_space=pltpu.VMEM)] * 2
+        + [pl.BlockSpec(memory_space=pltpu.MemorySpace.HBM)],
         out_specs=(pl.BlockSpec(memory_space=pltpu.VMEM),) * 2,
         scratch_shapes=scratch,
         compiler_params=pltpu.CompilerParams(
@@ -401,8 +450,8 @@
     grad, total = fused(gate, acts, weights, samples, sizes)
     input_grad = grad.reshape(activations.shape)
     unit = offsets * chan_in // ROWS
-    weight_grad = total[:unit].astype(jnp.float32).reshape(offsets, chan_in, chan_out)
-    bias = total[unit].astype(jnp.float32)
+    weight_grad = decode(total[:unit]).reshape(offsets, chan_in, chan_out)
+    bias = decode(total[unit])
     return (input_grad, weight_grad, bias[0] + bias[1])
 
 

time: 43.7 us -> 37.3 us (0.85)
  Pallas kernels: 35.8 us -> 29.5 us
    pallas_call x1, Pallas kernels: 35.8 us -> 29.5 us  [fused(): pl.pallas_call(functools.partial(body, sizes, parts, samples), out_shape=...]
    select_n x0 -> x2, other arithmetic: none -> 1.29 us  [decode(): return jnp.where(wide < 0, -root, root)]
    reshape x1 -> x0, other arithmetic: 1.01 us -> none  [on_device(): total[:unit].astype(jnp.float32).reshape(offsets, chan_in, chan_out)]
where the time goes in v2:
time: 37.3 us; the launch traced here: 37.1 us
  Pallas kernels  29.5 us (79%)
  local copies, waits for them, and re-layouts  4.05 us (11%)
  other arithmetic  2.83 us (8%)
  between operations  0.72 us (2%)
    pallas_call x1, Pallas kernels, fused(): pl.pallas_call(functools.partial(body, sizes, parts, samples), out_shape=...  29.5 us
    unnamed x6, local copies, waits for them, and re-layouts  2.1 us
    select_n x2, other arithmetic, decode(): return jnp.where(wide < 0, -root, root)  1.29 us
    reshape x1, local copies, waits for them, and re-layouts, on_device(): input_grad = grad.reshape(activations.shape)  0.87 us
    mul x1, other arithmetic, on_device(): jnp.repeat(jnp.repeat(jnp.repeat(upper, 2, 0), 2, 1), 2, 2)  0.79 us

profile of v2, /device:TPU:0, one launch (start us, length us, event | category | flops | bytes accessed | tf_op | source)
XLA Modules:
  0.0 37.1 jit_solution(3376567888722514622)
XLA Ops:
  0.6 0.8 %convert_multiply_fusion = f32[1,4,2,2048]{3,2,1,0:T(2,128)S(1)} fusion(bf16[1,4,2,2048]{3,2,1,0:T(2,128)(2,1)} %param.6), kind=kLoop, calls=%fused_computation.7 | loop fusion | flops 32768 | bytes 98304 | tf_op jit(solution)/shard_map/mul | solution.py:443
  1.4 0.1 reshape.49
  1.5 0.0 copy-start.1
  1.5 0.3 broadcast_in_dim.19
  1.8 0.7 %copy-done.1 = bf16[1,8,4,4096]{3,2,1,0:T(4,128)(2,1)S(1)} copy-done((bf16[1,8,4,4096]{3,2,1,0:T(4,128)(2,1)S(1)}, bf16[1,8,4,4096]{3,2,1,0:T(4,128)(2,1)}, u32[]{:S(2)}) %copy-start.1) | copy-done | bytes 262168
  2.5 0.1 compare_select_fusion
  2.6 0.4 select_n.16
  3.0 0.0 copy-start.2
  3.0 0.1 multiply_convert_fusion.gate_ref
  3.1 0.8 %copy-done.2 = bf16[1,8,4,2048]{3,2,1,0:T(4,128)(2,1)S(1)} copy-done((bf16[1,8,4,2048]{3,2,1,0:T(4,128)(2,1)S(1)}, bf16[1,8,4,2048]{3,2,1,0:T(4,128)(2,1)}, u32[]{:S(2)}) %copy-start.2) | copy-done | bytes 131096
  3.9 0.0 copy-start
  3.9 0.3 reshape.44
  4.2 0.1 copy.7
  4.3 0.6 %copy-done = bf16[27,64,128]{2,1,0:T(8,128)(2,1)S(1)} copy-done((bf16[27,64,128]{2,1,0:T(8,128)(2,1)S(1)}, bf16[27,64,128]{2,1,0:T(8,128)(2,1)}, u32[]{:S(2)}) %copy-start) | copy-done | bytes 442392
  4.9 29.5 %shard_map.67 = (bf16[1024,64]{1,0:T(8,128)(2,1)S(1)}, bf16[224,8,128]{2,1,0:T(8,128)(2,1)S(1)}) custom-call(bf16[8,4,32,128]{3,2,1,0:T(8,128)(2,1)S(1)} %multiply_convert_fusion.gate_ref, bf16[64,1024]{1,0:T(8,128)(2,1)S(1)} %bitcast.15, bf16[27,64,128]{2,1,0:T(8,128)(2,1)S(1)} %copy-done), custom_call_target="tpu_custom_call" | custom-call | tf_op jit(solution)/shard_map/pallas_call | solution.py:420
  34.4 0.9 %reshape.45 = bf16[1,8,4,2048]{3,2,1,0:T(4,128)(2,1)} reshape(bf16[1024,64]{1,0:T(8,128)(2,1)S(1)} %get-tuple-element.5) | data formatting | bytes 262144 | tf_op jit(solution)/shard_map/reshape | solution.py:451
  35.2 1.3 %negate_select_fusion = f32[216,8,128]{2,1,0:T(8,128)} fusion(bf16[224,8,128]{2,1,0:T(8,128)(2,1)S(1)} %get-tuple-element.6), kind=kLoop, calls=%fused_computation | loop fusion | flops 1327104 | bytes 1327104 | tf_op jit(solution)/shard_map/jit(_where)/select_n | solution.py:114
  36.5 0.5 %add_bitcast_fusion = f32[128]{0:T(128)} fusion(f32[8,128]{1,0:T(8,128)S(1)} %negate_select_fusion.1), kind=kLoop, calls=%fused_computation.15 | loop fusion | flops 128 | bytes 1536 | tf_op jit(solution)/shard_map/add | solution.py:455
  (3 shorter events, 0.0 us)
Async XLA Ops:
  1.5 1.0 %copy-start.1 = (bf16[1,8,4,4096]{3,2,1,0:T(4,128)(2,1)S(1)}, bf16[1,8,4,4096]{3,2,1,0:T(4,128)(2,1)}, u32[]{:S(2)}) copy-start(bf16[1,8,4,4096]{3,2,1,0:T(4,128)(2,1)} %param.5) | copy-start | bytes 786436
  3.0 0.9 %copy-start.2 = (bf16[1,8,4,2048]{3,2,1,0:T(4,128)(2,1)S(1)}, bf16[1,8,4,2048]{3,2,1,0:T(4,128)(2,1)}, u32[]{:S(2)}) copy-start(bf16[1,8,4,2048]{3,2,1,0:T(4,128)(2,1)} %param.4) | copy-start | bytes 393220
  3.9 1.0 %copy-start = (bf16[27,64,128]{2,1,0:T(8,128)(2,1)S(1)}, bf16[27,64,128]{2,1,0:T(8,128)(2,1)}, u32[]{:S(2)}) copy-start(bf16[27,64,128]{2,1,0:T(8,128)(2,1)} %weights_hbm.1) | copy-start | bytes 1327108

commit v3 on v2

--- a/solution.py
+++ b/solution.py
@@ -14,10 +14,7 @@
 
 
 FACTORS = ("core", "chip", "sx", "sy")
-GROUPS = (
-    (("core", "chip", "sx"), ("sy",)),
-    (("core", "sy"), ("chip", "sx")),
-)
+GROUPS = ((("core","chip","sx"), ("sy",)), (("core","sy"),("chip","sx")), (("core","chip","sx"), ("sy",)),)
 CODE = 2.0**36
 
 

time: 37.3 us -> 35.8 us (0.960)
  Pallas kernels: 29.5 us -> 27.9 us
    pallas_call x1, Pallas kernels: 29.5 us -> 27.9 us  [fused(): pl.pallas_call(functools.partial(body, sizes, parts, samples), out_shape=...]
where the time goes in v3:
time: 35.8 us; the launch traced here: 35.5 us
  Pallas kernels  27.9 us (78%)
  local copies, waits for them, and re-layouts  4.05 us (11%)
  other arithmetic  2.83 us (8%)
  between operations  0.72 us (2%)
    pallas_call x1, Pallas kernels, fused(): pl.pallas_call(functools.partial(body, sizes, parts, samples), out_shape=...  27.9 us
    unnamed x6, local copies, waits for them, and re-layouts  2.1 us
    select_n x2, other arithmetic, decode(): return jnp.where(wide < 0, -root, root)  1.29 us
    reshape x1, local copies, waits for them, and re-layouts, on_device(): input_grad = grad.reshape(activations.shape)  0.87 us
    mul x1, other arithmetic, on_device(): jnp.repeat(jnp.repeat(jnp.repeat(upper, 2, 0), 2, 1), 2, 2)  0.79 us

profile of v3, /device:TPU:0, one launch (start us, length us, event | category | flops | bytes accessed | tf_op | source)
XLA Modules:
  0.0 35.5 jit_solution(8958920770468652924)
XLA Ops:
  0.6 0.8 %convert_multiply_fusion = f32[1,4,2,2048]{3,2,1,0:T(2,128)S(1)} fusion(bf16[1,4,2,2048]{3,2,1,0:T(2,128)(2,1)} %param.6), kind=kLoop, calls=%fused_computation.7 | loop fusion | flops 32768 | bytes 98304 | tf_op jit(solution)/shard_map/mul | solution.py:440
  1.4 0.1 reshape.49
  1.5 0.0 copy-start.1
  1.5 0.3 broadcast_in_dim.19
  1.8 0.7 %copy-done.1 = bf16[1,8,4,4096]{3,2,1,0:T(4,128)(2,1)S(1)} copy-done((bf16[1,8,4,4096]{3,2,1,0:T(4,128)(2,1)S(1)}, bf16[1,8,4,4096]{3,2,1,0:T(4,128)(2,1)}, u32[]{:S(2)}) %copy-start.1) | copy-done | bytes 262168
  2.5 0.1 compare_select_fusion
  2.6 0.4 %select_n.16 = f32[8,4,32,128]{3,2,1,0:T(8,128)S(1)} reshape(f32[1,8,4,4096]{3,2,1,0:T(4,128)S(1)} %compare_select_fusion) | data formatting | bytes 1048576 | tf_op jit(solution)/shard_map/jit(_where)/select_n | solution.py:442
  3.0 0.0 copy-start.2
  3.0 0.1 multiply_convert_fusion.gate_ref
  3.1 0.8 %copy-done.2 = bf16[1,8,4,2048]{3,2,1,0:T(4,128)(2,1)S(1)} copy-done((bf16[1,8,4,2048]{3,2,1,0:T(4,128)(2,1)S(1)}, bf16[1,8,4,2048]{3,2,1,0:T(4,128)(2,1)}, u32[]{:S(2)}) %copy-start.2) | copy-done | bytes 131096
  3.9 0.0 copy-start
  3.9 0.3 reshape.44
  4.2 0.1 copy.7
  4.3 0.6 %copy-done = bf16[27,64,128]{2,1,0:T(8,128)(2,1)S(1)} copy-done((bf16[27,64,128]{2,1,0:T(8,128)(2,1)S(1)}, bf16[27,64,128]{2,1,0:T(8,128)(2,1)}, u32[]{:S(2)}) %copy-start) | copy-done | bytes 442392
  4.9 27.9 %shard_map.67 = (bf16[1024,64]{1,0:T(8,128)(2,1)S(1)}, bf16[224,8,128]{2,1,0:T(8,128)(2,1)S(1)}) custom-call(bf16[8,4,32,128]{3,2,1,0:T(8,128)(2,1)S(1)} %multiply_convert_fusion.gate_ref, bf16[64,1024]{1,0:T(8,128)(2,1)S(1)} %bitcast.15, bf16[27,64,128]{2,1,0:T(8,128)(2,1)S(1)} %copy-done), custom_call_target="tpu_custom_call" | custom-call | tf_op jit(solution)/shard_map/pallas_call | solution.py:417
  32.8 0.9 %reshape.45 = bf16[1,8,4,2048]{3,2,1,0:T(4,128)(2,1)} reshape(bf16[1024,64]{1,0:T(8,128)(2,1)S(1)} %get-tuple-element.5) | data formatting | bytes 262144 | tf_op jit(solution)/shard_map/reshape | solution.py:448
  33.7 1.3 %negate_select_fusion = f32[216,8,128]{2,1,0:T(8,128)} fusion(bf16[224,8,128]{2,1,0:T(8,128)(2,1)S(1)} %get-tuple-element.6), kind=kLoop, calls=%fused_computation | loop fusion | flops 1327104 | bytes 1327104 | tf_op jit(solution)/shard_map/jit(_where)/select_n | solution.py:111
  35.0 0.5 %add_bitcast_fusion = f32[128]{0:T(128)} fusion(f32[8,128]{1,0:T(8,128)S(1)} %negate_select_fusion.1), kind=kLoop, calls=%fused_computation.15 | loop fusion | flops 128 | bytes 1536 | tf_op jit(solution)/shard_map/add | solution.py:452
  (3 shorter events, 0.0 us)
Async XLA Ops:
  1.5 1.0 %copy-start.1 = (bf16[1,8,4,4096]{3,2,1,0:T(4,128)(2,1)S(1)}, bf16[1,8,4,4096]{3,2,1,0:T(4,128)(2,1)}, u32[]{:S(2)}) copy-start(bf16[1,8,4,4096]{3,2,1,0:T(4,128)(2,1)} %param.5) | copy-start | bytes 786436
  3.0 0.9 %copy-start.2 = (bf16[1,8,4,2048]{3,2,1,0:T(4,128)(2,1)S(1)}, bf16[1,8,4,2048]{3,2,1,0:T(4,128)(2,1)}, u32[]{:S(2)}) copy-start(bf16[1,8,4,2048]{3,2,1,0:T(4,128)(2,1)} %param.4) | copy-start | bytes 393220
  3.9 1.0 %copy-start = (bf16[27,64,128]{2,1,0:T(8,128)(2,1)S(1)}, bf16[27,64,128]{2,1,0:T(8,128)(2,1)}, u32[]{:S(2)}) copy-start(bf16[27,64,128]{2,1,0:T(8,128)(2,1)} %weights_hbm.1) | copy-start | bytes 1327108
